TPU v7x, 256 devices: a whole 4x4x8 slice. The times are simulated.
256 devices in a mesh: ent: 64 (over z, x, core), basis: 4 (over y).
Axes of the slice: x: 4, y: 4, z: 8, core: 2. Of those that a mesh axis runs over, the one named last changes fastest.
Arguments:
- entity_rows: bfloat16 [32768, 256], P('ent'), may hold values from -6 to 6
- self_weight: bfloat16 [256, 256], replicated, may hold values from -0.375 to 0.375
- bases: bfloat16 [32, 256, 256], P('basis'), may hold values from -0.375 to 0.375
- coefficients: float32 [1315, 32], P(None, 'basis'), may hold values from -1 to 1
- send_block: int32 [64, 64, 2], P('ent'), may hold values from 0 to 3
- edge_rel: int32 [64, 64, 2], P('ent'), may hold values from 0 to 1314
- edge_dst: int32 [64, 64, 2], P(None, 'ent'), may hold values from 0 to 3
- edge_count: int32 [64, 64, 2], P(None, 'ent'), may hold values from 0 to 128, as said below
- cotangent: bfloat16 [32768, 256], P('ent'), may hold values from -0.75 to 0.75
Outputs:
- activation: bfloat16 [32768, 256], P('ent', 'basis')
- basis_grad: float32 [32, 256, 256], P('basis', 'ent')
- coef_grad: float32 [1315, 32], P(None, 'basis')
- entity_grad: bfloat16 [32768, 256], P('ent', 'basis')
Inputs may be any that keep to these rules, and one draw needn't show every extreme that they name: `edge_count`: 0 marks an empty slot; every draw has slots with all 128 rows live.
All inputs are finite; a program needn't handle non-finite values.
Results may differ from a plain program's by a relative error of at most 0.015.
Values may be sent and summed in bfloat16 or wider, within the bound.
No kernel may reach another device: no remote copies, remote signals or barrier semaphores. Data moves between devices by JAX's collectives and lax.ppermute only.
A program may use at most 128 MiB of HBM per device.

v0:
```python
import jax
import jax.numpy as jnp
from jax import lax
from jax.sharding import PartitionSpec as P

BLK = 128


def silu_parts(values):
    logistic = jax.nn.sigmoid(values)
    return (values * logistic, logistic * (1.0 + values * (1.0 - logistic)))


def local(
    entity_rows,
    self_weight,
    bases,
    coefficients,
    send_block,
    edge_rel,
    edge_dst,
    edge_count,
    cotangent,
):
    peers = lax.axis_size("ent")
    groups = lax.axis_size("basis")
    group_index = lax.axis_index("basis")
    ent_dev, feature_width = entity_rows.shape
    block_count = ent_dev // BLK
    share_width = feature_width // groups
    own_bases = bases.shape[0]
    col_start = group_index * share_width
    blocks = entity_rows.reshape(block_count, BLK, feature_width)
    outgoing = jnp.take(blocks, send_block[0], axis=0)
    outgoing_rel = edge_rel[0]
    incoming, rel_in = (
        lax.all_to_all(outgoing, "ent", split_axis=0, concat_axis=0, tiled=True),
        lax.all_to_all(outgoing_rel, "ent", split_axis=0, concat_axis=0, tiled=True),
    )
    slot_count = peers * incoming.shape[1]
    dst_local = edge_dst[:, 0, :]
    row_iota = lax.broadcasted_iota(jnp.int32, (1, 1, BLK), 2)
    live_rows = row_iota < edge_count[:, 0, :][:, :, None]
    incoming = jnp.where(live_rows[..., None], incoming, jnp.zeros((), jnp.bfloat16))
    coef_bf = coefficients.astype(jnp.bfloat16)
    in_weights = jnp.take(coef_bf, rel_in.reshape(slot_count), axis=0)
    block_iota = lax.broadcasted_iota(jnp.int32, (1, block_count), 1)
    target_hot = (dst_local.reshape(slot_count)[:, None] == block_iota).astype(jnp.bfloat16)
    spread = (target_hot[:, :, None] * in_weights[:, None, :]).reshape(
        slot_count, block_count * own_bases
    )
    flat_in = incoming.reshape(slot_count, BLK * feature_width)
    messages = lax.dot_general(
        spread, flat_in, (((0,), (0,)), ((), ())), preferred_element_type=jnp.float32
    )
    messages = messages.astype(jnp.bfloat16).reshape(block_count, own_bases, BLK, feature_width)
    partial_sum = jnp.einsum(
        "kbrd,bde->kre", messages, bases, preferred_element_type=jnp.float32
    ).reshape(ent_dev, feature_width)
    aggregate = lax.psum(partial_sum, "basis")
    pre_act = jnp.dot(entity_rows, self_weight, preferred_element_type=jnp.float32) + aggregate
    activated, slope_value = silu_parts(pre_act)
    pre_grad = (cotangent.astype(jnp.float32) * slope_value).astype(jnp.bfloat16)
    activation = lax.dynamic_slice_in_dim(activated, col_start, share_width, 1).astype(jnp.bfloat16)
    grad_blocks = pre_grad.reshape(block_count, BLK, feature_width)
    basis_term = jnp.einsum(
        "kbrd,kre->bde", messages, grad_blocks, preferred_element_type=jnp.float32
    )
    basis_grad = lax.psum_scatter(basis_term, "ent", scatter_dimension=1, tiled=True)
    back_blocks = jnp.take(grad_blocks, dst_local, axis=0)
    back_blocks = jnp.where(live_rows[..., None], back_blocks, jnp.zeros((), jnp.bfloat16))
    returned_in = lax.all_to_all(back_blocks, "ent", split_axis=0, concat_axis=0, tiled=True)
    src_local = send_block[0].reshape(slot_count)
    rel_local = edge_rel[0].reshape(slot_count)
    out_weights = jnp.take(coef_bf, rel_local, axis=0)
    source_hot = (src_local[:, None] == block_iota).astype(jnp.bfloat16)
    spread_back = (source_hot[:, :, None] * out_weights[:, None, :]).reshape(
        slot_count, block_count * own_bases
    )
    flat_back = returned_in.reshape(slot_count, BLK * feature_width)
    returned = lax.dot_general(
        spread_back, flat_back, (((0,), (0,)), ((), ())), preferred_element_type=jnp.float32
    )
    returned = returned.astype(jnp.bfloat16).reshape(block_count, own_bases, BLK, feature_width)
    back_partial = jnp.einsum(
        "kbre,bde->krd", returned, bases, preferred_element_type=jnp.float32
    ).reshape(ent_dev, feature_width)
    back_share = lax.psum_scatter(
        back_partial.astype(jnp.bfloat16), "basis", scatter_dimension=1, tiled=True
    ).astype(jnp.float32)
    weight_rows = lax.dynamic_slice_in_dim(self_weight, col_start, share_width, 0)
    self_part = lax.dot_general(
        pre_grad, weight_rows, (((1,), (1,)), ((), ())), preferred_element_type=jnp.float32
    )
    entity_grad = (self_part + back_share).astype(jnp.bfloat16)
    projected = jnp.einsum(
        "nd,bde->bne", entity_rows, bases, preferred_element_type=jnp.float32
    ).astype(jnp.bfloat16)
    proj_flat = projected.reshape(own_bases * block_count, BLK * feature_width)
    scores = lax.dot_general(
        flat_back, proj_flat, (((1,), (1,)), ((), ())), preferred_element_type=jnp.float32
    )
    scores = scores.reshape(slot_count, own_bases, block_count)
    per_slot = jnp.sum(scores * source_hot.astype(jnp.float32)[:, None, :], axis=2)
    relation_iota = lax.broadcasted_iota(jnp.int32, (1, coefficients.shape[0]), 1)
    relation_hot = (rel_local[:, None] == relation_iota).astype(jnp.float32)
    coef_term = lax.dot_general(
        relation_hot,
        per_slot,
        (((0,), (0,)), ((), ())),
        precision=lax.Precision.HIGHEST,
        preferred_element_type=jnp.float32,
    )
    coef_grad = lax.psum(coef_term, "ent")
    return (activation, basis_grad, coef_grad, entity_grad)


def solution(mesh):
    placed = (
        P("ent", None),
        P(),
        P("basis", None, None),
        P(None, "basis"),
        P("ent", None, None),
        P("ent", None, None),
        P(None, "ent", None),
        P(None, "ent", None),
        P("ent", None),
    )
    return jax.shard_map(
        local,
        mesh=mesh,
        in_specs=placed,
        out_specs=(P("ent", "basis"), P("basis", "ent", None), P(None, "basis"), P("ent", "basis")),
        check_vma=False,
    )
```

profile of v0, /device:TPU:16, one launch (start us, length us, event | category | flops | bytes accessed | tf_op | source)
XLA Modules:
  0.0 820.5 jit_solution(8115167516258157078)
XLA Ops:
  7.2 1.5 copy.69
  8.7 11.9 %all-to-all-start = ((s32[64,1,2]{2,1,0:T(1,128)}), s32[64,1,2]{2,1,0:T(1,128)S(1)}, u32[]{:S(2)}, u32[]{:S(2)}) async-start(s32[64,1,2]{2,1,0:T(1,128)} %copy.69), calls=%async_computation | async-start | bytes 65536 | tf_op jit(solution)/shard_map/all_to_all | solution.py:38
  20.6 0.7 compare_and_fusion.1
  21.3 0.7 compare_select_fusion
  22.2 0.1 reshape.202
  22.4 7.5 gather_fusion.1
  29.8 7.4 broadcast_select_fusion
  37.3 10.6 %all-to-all-start.1 = ((bf16[64,2,128,256]{3,2,1,0:T(8,128)(2,1)}), bf16[64,2,128,256]{3,2,1,0:T(8,128)(2,1)}, u32[]{:S(2)}, u32[]{:S(2)}) async-start(bf16[64,2,128,256]{3,2,1,0:T(8,128)(2,1)} %broadcast_select_fusion), calls=%async_computation.1 | async-start | bytes 16777216 | tf_op jit(solution)/shard_map/all_to_all | solution.py:37
  47.9 0.2 all-reduce.2.cloned.1.call-start
  48.3 0.1 eq.57
  48.5 0.2 copy.70
  48.9 0.5 broadcast.90
  49.4 0.7 reduce.3
  50.3 0.7 gather_fusion
  51.1 182.8 %all-to-all-done.1 = bf16[64,2,128,256]{3,2,1,0:T(8,128)(2,1)} async-done(((bf16[64,2,128,256]{3,2,1,0:T(8,128)(2,1)}), bf16[64,2,128,256]{3,2,1,0:T(8,128)(2,1)}, u32[]{:S(2)}, u32[]{:S(2)}) %all-to-all-start.1) | async-done | bytes 8388640 | tf_op jit(solution)/shard_map/all_to_all | solution.py:37
  234.0 8.0 broadcast_select_fusion.1
  242.0 12.3 %copy.94 = bf16[16,8,128,256]{3,1,2,0:T(8,128)(2,1)} copy(bf16[16,8,128,256]{3,2,1,0:T(8,128)(2,1)} %bitcast.74) | data formatting | bytes 16777216
  254.3 4.7 convolution_convert_fusion.1
  259.0 1.3 copy-done.2
  260.3 0.5 copy.75
  260.8 1.5 convolution_bitcast_fusion.2
  262.6 0.1 reshape.206
  262.7 44.4 %all-reduce.2.cloned.1.call-done = f32[512,256]{1,0:T(8,128)} async-done(((f32[512,256]{1,0:T(8,128)}), f32[512,256]{1,0:T(8,128)}) %all-reduce.2.cloned.1.call-update) | async-done | bytes 524304 | tf_op jit(solution)/shard_map/psum | solution.py:60
  307.2 2.4 multiply_convert_fusion
  309.6 6.4 gather_fusion.2
  316.0 8.0 select_select_fusion
  324.0 10.7 %all-to-all-start.2 = ((bf16[64,2,128,256]{3,2,1,0:T(8,128)(2,1)}), bf16[64,2,128,256]{3,2,1,0:T(8,128)(2,1)}, u32[]{:S(2)}, u32[]{:S(2)}) async-start(bf16[64,2,128,256]{3,2,1,0:T(8,128)(2,1)} %select_select_fusion), calls=%async_computation.3 | async-start | bytes 16777216 | tf_op jit(solution)/shard_map/all_to_all | solution.py:72
  334.8 4.8 copy.89
  339.6 3.6 convolution_bitcast_fusion
  343.7 0.1 eq.65
  343.8 0.7 gather_fusion.3
  344.7 2.1 convert_bitcast_fusion
  346.8 2.8 copy.82
  349.7 2.8 dot_general.47
  352.5 1.2 fusion.12
  353.7 0.7 copy.87
  354.4 158.4 %reduce-scatter.3.cloned.1.call-done = f32[8,4,256]{2,0,1:T(8,128)} async-done(((f32[8,256,256]{2,0,1:T(8,128)}), f32[8,4,256]{2,0,1:T(8,128)}) %reduce-scatter.3.cloned.1.call-update) | async-done | bytes 32784 | tf_op jit(solution)/shard_map/reduce_scatter | solution.py:69
  512.8 1.4 copy.88
  514.2 12.7 %all-to-all-done.2 = bf16[64,2,128,256]{3,2,1,0:T(8,128)(2,1)} async-done(((bf16[64,2,128,256]{3,2,1,0:T(8,128)(2,1)}), bf16[64,2,128,256]{3,2,1,0:T(8,128)(2,1)}, u32[]{:S(2)}, u32[]{:S(2)}) %all-to-all-start.2) | async-done | bytes 8388640 | tf_op jit(solution)/shard_map/all_to_all | solution.py:72
  526.9 12.4 %copy.95 = bf16[16,8,128,256]{3,1,2,0:T(8,128)(2,1)} copy(bf16[16,8,128,256]{3,2,1,0:T(8,128)(2,1)} %bitcast.31) | data formatting | bytes 16777216
  539.3 4.6 convolution_convert_fusion
  543.9 0.5 copy.86
  544.4 1.4 fusion.2
  545.8 13.6 %reshape.216 = bf16[128,32768,1]{1,0,2:T(8,128)(2,1)} reshape(bf16[64,2,128,256]{3,2,1,0:T(8,128)(2,1)} %all-to-all-done.2) | data formatting | bytes 16777216 | tf_op jit(solution)/shard_map/reshape | solution.py:80
  559.5 6.2 fusion.7
  565.7 0.4 fusion.10
  566.1 246.2 %psum.15 = f32[1315,8]{0,1:T(8,128)} all-reduce(f32[1315,8]{0,1:T(8,128)S(1)} %fusion.10), channel_id=1, replica_groups=mesh['ent'=64,'basis'=4] {'ent'}, use_global_device_ids=true, to_apply=%region_3.6 | all-reduce | flops 10520 | bytes 84160 | tf_op jit(solution)/shard_map/psum | solution.py:114
  812.3 1.7 fusion.3
  (53 shorter events, 1.8 us)
Async XLA Ops:
  7.2 253.6 %copy-start = (bf16[8,256,256]{2,1,0:T(8,128)(2,1)S(1)}, bf16[8,256,256]{2,1,0:T(8,128)(2,1)}, u32[]{:S(2)}) copy-start(bf16[8,256,256]{2,1,0:T(8,128)(2,1)} %param.15) | copy-start | bytes 3145732
  8.7 28.6 %all-to-all-start = ((s32[64,1,2]{2,1,0:T(1,128)}), s32[64,1,2]{2,1,0:T(1,128)S(1)}, u32[]{:S(2)}, u32[]{:S(2)}) async-start(s32[64,1,2]{2,1,0:T(1,128)} %copy.69), calls=%async_computation | async-start | bytes 65536 | tf_op jit(solution)/shard_map/all_to_all | solution.py:38
  37.3 10.9 %copy-start.5 = (s32[64,1,2]{0,2,1:T(2,128)S(1)}, s32[64,1,2]{0,2,1:T(2,128)}, u32[]{:S(2)}) copy-start(s32[64,1,2]{0,2,1:T(2,128)} %param.19) | copy-start | bytes 1540
  37.3 11.0 %copy-start.9 = (s32[64,1,2]{0,2,1:T(2,128)S(1)}, s32[64,1,2]{0,2,1:T(2,128)}, u32[]{:S(2)}) copy-start(s32[64,1,2]{0,2,1:T(2,128)} %param.20) | copy-start | bytes 1540
  37.3 11.2 %copy-start.4 = (f32[1315,8]{0,1:T(8,128)S(1)}, f32[1315,8]{0,1:T(8,128)}, u32[]{:S(2)}) copy-start(f32[1315,8]{0,1:T(8,128)} %param.16) | copy-start | bytes 126244
  37.3 196.7 %all-to-all-start.1 = ((bf16[64,2,128,256]{3,2,1,0:T(8,128)(2,1)}), bf16[64,2,128,256]{3,2,1,0:T(8,128)(2,1)}, u32[]{:S(2)}, u32[]{:S(2)}) async-start(bf16[64,2,128,256]{3,2,1,0:T(8,128)(2,1)} %broadcast_select_fusion), calls=%async_computation.1 | async-start | bytes 16777216 | tf_op jit(solution)/shard_map/all_to_all | solution.py:37
  47.9 259.3 %all-reduce.2.cloned.1.call-start = ((), (), s32[]{:S(2)}) async-start(), calls=%async_computation.5 | async-start | bytes 1048576 | tf_op jit(solution)/shard_map/psum | solution.py:60
  254.3 52.9 %copy-start.1 = (bf16[512,256]{1,0:T(8,128)(2,1)S(1)}, bf16[512,256]{1,0:T(8,128)(2,1)}, u32[]{:S(2)}) copy-start(bf16[512,256]{1,0:T(8,128)(2,1)} %param.13) | copy-start | bytes 786436
  254.3 52.9 %copy-start.7 = (bf16[256,256]{1,0:T(8,128)(2,1)S(1)}, bf16[256,256]{1,0:T(8,128)(2,1)}, u32[]{:S(2)}) copy-start(bf16[256,256]{1,0:T(8,128)(2,1)} %param.14) | copy-start | bytes 393220
  254.3 52.9 %copy-start.10 = (bf16[512,256]{1,0:T(8,128)(2,1)S(1)}, bf16[512,256]{1,0:T(8,128)(2,1)}, u32[]{:S(2)}) copy-start(bf16[512,256]{1,0:T(8,128)(2,1)} %param.21) | copy-start | bytes 786436
  259.0 1.3 copy-start.2
  324.0 202.9 %all-to-all-start.2 = ((bf16[64,2,128,256]{3,2,1,0:T(8,128)(2,1)}), bf16[64,2,128,256]{3,2,1,0:T(8,128)(2,1)}, u32[]{:S(2)}, u32[]{:S(2)}) async-start(bf16[64,2,128,256]{3,2,1,0:T(8,128)(2,1)} %select_select_fusion), calls=%async_computation.3 | async-start | bytes 16777216 | tf_op jit(solution)/shard_map/all_to_all | solution.py:72
  334.7 8.6 %copy-start.8 = (s32[1,64,2]{1,2,0:T(2,128)S(1)}, s32[1,64,2]{1,2,0:T(2,128)}, u32[]{:S(2)}) copy-start(s32[1,64,2]{1,2,0:T(2,128)} %param.18) | copy-start | bytes 1540
  334.7 8.7 %copy-start.6 = (s32[1,64,2]{1,2,0:T(2,128)S(1)}, s32[1,64,2]{1,2,0:T(2,128)}, u32[]{:S(2)}) copy-start(s32[1,64,2]{1,2,0:T(2,128)} %param.17) | copy-start | bytes 1540
  334.7 178.1 %reduce-scatter.3.cloned.1.call-start = ((), (), s32[]{:S(2)}) async-start(), calls=%async_computation.6 | async-start | bytes 2129920 | tf_op jit(solution)/shard_map/reduce_scatter | solution.py:69
  343.3 469.0 %reduce-scatter.5.cloned.1.call-start = ((), (), s32[]{:S(2)}) async-start(), calls=%async_computation.7 | async-start | bytes 327680 | tf_op jit(solution)/shard_map/reduce_scatter | solution.py:88
  545.8 13.7 %copy-start.3 = (bf16[8,4,32768]{2,1,0:T(4,128)(2,1)S(1)}, bf16[8,4,32768]{2,1,0:T(4,128)(2,1)}, u32[]{:S(2)}) copy-start(bf16[8,4,32768]{2,1,0:T(4,128)(2,1)} %dot_general.47) | copy-start | bytes 6291460
Sparse Core Ops, SparseCore 0:
  262.5 44.6 all-reduce.1
  343.4 169.3 reduce-scatter.2
  545.9 18.7 reduce-scatter.4
where the time goes:
time: 822 us; the launch traced here: 820 us
  waiting for transfers between devices  398 us (48%)
  blocking collectives  246 us (30%)
  local copies, waits for them, and re-layouts  72.5 us (9%)
  starting transfers between devices  33.5 us (4%)
  matrix products  28.6 us (3%)
  other arithmetic  27.2 us (3%)
  between operations  14 us (2%)
    psum x1, blocking collectives, local(): coef_grad = lax.psum(coef_term, 'ent')  246 us
    all_to_all x1, waiting for transfers between devices, local(): lax.all_to_all(outgoing, 'ent', split_axis=0, concat_axis=0, tiled=True)  183 us
    reduce_scatter x1, waiting for transfers between devices, local(): lax.psum_scatter(basis_term, 'ent', scatter_dimension=1, tiled=True)  158 us
    psum x1, waiting for transfers between devices, local(): aggregate = lax.psum(partial_sum, 'basis')  44.4 us
    unnamed x30, local copies, waits for them, and re-layouts  28.7 us
  transfers between devices with their start and end apart: 6, of which 4 were waited for; matrix products, arithmetic and copies ran while one was open for 7% of the time, Pallas kernels for 0%

commit v1 on v0

--- a/solution.py
+++ b/solution.py
@@ -111,7 +111,7 @@
         precision=lax.Precision.HIGHEST,
         preferred_element_type=jnp.float32,
     )
-    coef_grad = lax.psum(coef_term, "ent")
+    coef_grad = jnp.sum(lax.all_gather(coef_term, "ent"), axis=0)
     return (activation, basis_grad, coef_grad, entity_grad)
 
 

time: 822 us -> 659 us (0.80)
  blocking collectives: 246 us -> 0 us
  waiting for transfers between devices: 398 us -> 477 us
    psum x1 -> x0, blocking collectives: 246 us -> none  [local(): coef_grad = lax.psum(coef_term, 'ent')]
    all_to_all x1, waiting for transfers between devices: 12.7 us -> 174 us  [local(): lax.all_to_all(back_blocks, 'ent', split_axis=0, concat_axis=0, tiled=True)]
    reduce_scatter x1, waiting for transfers between devices: 158 us -> 0.01 us  [local(): lax.psum_scatter(basis_term, 'ent', scatter_dimension=1, tiled=True)]
    all_gather x0 -> x1, waiting for transfers between devices: none -> 75.1 us  [local(): coef_grad = jnp.sum(lax.all_gather(coef_term, 'ent'), axis=0)]
  transfers between devices with their start and end apart: 6 -> 7, of which waited for: 4 -> 4; matrix products, arithmetic and copies ran while one was open for 7% -> 13% of each run, Pallas kernels for 0% -> 0%
where the time goes in v1:
time: 659 us; the launch traced here: 657 us
  waiting for transfers between devices  477 us (72%)
  local copies, waits for them, and re-layouts  72.5 us (11%)
  starting transfers between devices  34 us (5%)
  other arithmetic  29.8 us (5%)
  matrix products  29.3 us (4%)
  between operations  14 us (2%)
    all_to_all x1, waiting for transfers between devices, local(): lax.all_to_all(outgoing, 'ent', split_axis=0, concat_axis=0, tiled=True)  183 us
    all_to_all x1, waiting for transfers between devices, local(): lax.all_to_all(back_blocks, 'ent', split_axis=0, concat_axis=0, tiled=True)  174 us
    all_gather x1, waiting for transfers between devices, local(): coef_grad = jnp.sum(lax.all_gather(coef_term, 'ent'), axis=0)  75.1 us
    psum x1, waiting for transfers between devices, local(): aggregate = lax.psum(partial_sum, 'basis')  44.4 us
    unnamed x30, local copies, waits for them, and re-layouts  28.7 us
    reshape x1, local copies, waits for them, and re-layouts, local(): flat_back = returned_in.reshape(slot_count, BLK * feature_width)  13.7 us
  transfers between devices with their start and end apart: 7, of which 4 were waited for; matrix products, arithmetic and copies ran while one was open for 13% of the time, Pallas kernels for 0%

profile of v1, /device:TPU:16, one launch (start us, length us, event | category | flops | bytes accessed | tf_op | source)
XLA Modules:
  0.0 656.5 jit_solution(11389768050291729461)
XLA Ops:
  7.2 1.5 copy.69
  8.7 11.9 %all-to-all-start = ((s32[64,1,2]{2,1,0:T(1,128)}), s32[64,1,2]{2,1,0:T(1,128)S(1)}, u32[]{:S(2)}, u32[]{:S(2)}) async-start(s32[64,1,2]{2,1,0:T(1,128)} %copy.69), calls=%async_computation | async-start | bytes 65536 | tf_op jit(solution)/shard_map/all_to_all | solution.py:38
  20.6 0.7 compare_and_fusion.1
  21.3 0.7 compare_select_fusion
  22.2 0.1 reshape.206
  22.4 7.5 %gather_fusion.1 = bf16[128,128,256]{2,1,0:T(8,128)(2,1)} fusion(bf16[4,128,256]{2,1,0:T(8,128)(2,1)} %bitcast.71, s32[1024]{0:T(1024)S(1)} %pad_clamp_fusion.2), kind=kCustom, calls=%fused_computation.1.clone | custom fusion | bytes 16777728 | tf_op jit(solution)/shard_map/jit(_take)/gather | solution.py:34
  29.8 7.4 %broadcast_select_fusion = bf16[64,2,128,256]{3,2,1,0:T(8,128)(2,1)} fusion(bf16[64,2,128,256]{3,2,1,0:T(8,128)(2,1)} %bitcast.74, pred[64,2]{1,0:T(8,128)(4,1)S(1)} %copy.73), kind=kLoop, calls=%fused_computation.7 | loop fusion | flops 4194304 | bytes 16777344 | tf_op jit(solution)/shard_map/jit(_take)/select_n | solution.py:34
  37.3 10.6 %all-to-all-start.1 = ((bf16[64,2,128,256]{3,2,1,0:T(8,128)(2,1)}), bf16[64,2,128,256]{3,2,1,0:T(8,128)(2,1)}, u32[]{:S(2)}, u32[]{:S(2)}) async-start(bf16[64,2,128,256]{3,2,1,0:T(8,128)(2,1)} %broadcast_select_fusion), calls=%async_computation.1 | async-start | bytes 16777216 | tf_op jit(solution)/shard_map/all_to_all | solution.py:37
  47.9 0.2 all-reduce.2.cloned.1.call-start
  48.5 0.2 copy.70
  48.9 0.5 broadcast.90
  49.4 0.7 reduce.4
  50.3 0.7 gather_fusion
  51.1 182.8 %all-to-all-done.1 = bf16[64,2,128,256]{3,2,1,0:T(8,128)(2,1)} async-done(((bf16[64,2,128,256]{3,2,1,0:T(8,128)(2,1)}), bf16[64,2,128,256]{3,2,1,0:T(8,128)(2,1)}, u32[]{:S(2)}, u32[]{:S(2)}) %all-to-all-start.1) | async-done | bytes 8388640 | tf_op jit(solution)/shard_map/all_to_all | solution.py:37
  234.0 8.0 %broadcast_select_fusion.1 = bf16[64,2,128,256]{3,2,1,0:T(8,128)(2,1)} fusion(bf16[64,2,128,256]{3,2,1,0:T(8,128)(2,1)} %all-to-all-done.1, pred[64,2,128]{2,1,0:T(4,128)(4,1)S(1)} %iota_compare_fusion.2), kind=kLoop, calls=%fused_computation.8 | loop fusion | flops 4194304 | bytes 16793600 | tf_op jit(solution)/shard_map/jit(_where)/select_n | solution.py:44
  242.0 12.3 %copy.94 = bf16[16,8,128,256]{3,1,2,0:T(8,128)(2,1)} copy(bf16[16,8,128,256]{3,2,1,0:T(8,128)(2,1)} %bitcast.76) | data formatting | bytes 16777216
  254.3 4.7 convolution_convert_fusion.1
  259.0 1.3 copy-done.2
  260.3 0.5 copy.75
  260.8 1.5 convolution_bitcast_fusion.3
  262.6 0.1 reshape.210
  262.7 44.4 %all-reduce.2.cloned.1.call-done = f32[512,256]{1,0:T(8,128)} async-done(((f32[512,256]{1,0:T(8,128)}), f32[512,256]{1,0:T(8,128)}) %all-reduce.2.cloned.1.call-update) | async-done | bytes 524304 | tf_op jit(solution)/shard_map/psum | solution.py:60
  307.1 2.4 multiply_convert_fusion
  309.5 6.4 gather_fusion.2
  315.9 8.1 %select_select_fusion = bf16[64,2,128,256]{3,2,1,0:T(8,128)(2,1)} fusion(bf16[64,2,128,256]{3,2,1,0:T(8,128)(2,1)} %bitcast.73, pred[64,2]{1,0:T(8,128)(4,1)S(1)} %copy.79, pred[64,2,128]{2,1,0:T(4,128)(4,1)S(1)} %iota_compare_fusion.2), kind=kLoop, calls=%fused_computation.6 | loop fusion | flops 8388608 | bytes 16793728 | tf_op jit(solution)/shard_map/jit(_where)/select_n | solution.py:71
  324.0 10.9 %all-to-all-start.2 = ((bf16[64,2,128,256]{3,2,1,0:T(8,128)(2,1)}), bf16[64,2,128,256]{3,2,1,0:T(8,128)(2,1)}, u32[]{:S(2)}, u32[]{:S(2)}) async-start(bf16[64,2,128,256]{3,2,1,0:T(8,128)(2,1)} %select_select_fusion), calls=%async_computation.3 | async-start | bytes 16777216 | tf_op jit(solution)/shard_map/all_to_all | solution.py:72
  335.0 4.8 copy.89
  339.8 3.6 convolution_bitcast_fusion.1
  343.8 0.1 eq.65
  344.0 0.7 gather_fusion.3
  344.9 2.1 convert_bitcast_fusion
  347.0 2.8 copy.82
  349.9 2.8 dot_general.47
  352.6 174.4 %all-to-all-done.2 = bf16[64,2,128,256]{3,2,1,0:T(8,128)(2,1)} async-done(((bf16[64,2,128,256]{3,2,1,0:T(8,128)(2,1)}), bf16[64,2,128,256]{3,2,1,0:T(8,128)(2,1)}, u32[]{:S(2)}, u32[]{:S(2)}) %all-to-all-start.2) | async-done | bytes 8388640 | tf_op jit(solution)/shard_map/all_to_all | solution.py:72
  527.1 12.4 %copy.95 = bf16[16,8,128,256]{3,1,2,0:T(8,128)(2,1)} copy(bf16[16,8,128,256]{3,2,1,0:T(8,128)(2,1)} %bitcast.32) | data formatting | bytes 16777216
  539.4 4.6 convolution_convert_fusion
  544.0 0.5 copy.86
  544.5 1.5 fusion.2
  546.0 0.3 all-gather.4.cloned.1.call-start
  546.4 13.7 %reshape.220 = bf16[128,32768,1]{1,0,2:T(8,128)(2,1)} reshape(bf16[64,2,128,256]{3,2,1,0:T(8,128)(2,1)} %all-to-all-done.2) | data formatting | bytes 16777216 | tf_op jit(solution)/shard_map/reshape | solution.py:80
  560.0 6.2 fusion.7
  566.2 1.0 convolution_bitcast_fusion
  567.3 1.2 fusion.11
  568.5 0.7 copy.87
  569.2 1.4 copy.88
  570.6 1.7 fusion.3
  572.3 75.1 %all-gather.4.cloned.1.call-done = f32[64,1315,8]{1,2,0:T(8,128)} async-done(((f32[1,1315,8]{1,2,0:T(8,128)}), f32[64,1315,8]{1,2,0:T(8,128)}) %all-gather.4.cloned.1.call-update) | async-done | bytes 2693136 | tf_op jit(solution)/shard_map/all_gather | solution.py:114
  647.4 2.6 reduce_sum.19
  (56 shorter events, 1.9 us)
Async XLA Ops:
  7.2 253.7 %copy-start = (bf16[8,256,256]{2,1,0:T(8,128)(2,1)S(1)}, bf16[8,256,256]{2,1,0:T(8,128)(2,1)}, u32[]{:S(2)}) copy-start(bf16[8,256,256]{2,1,0:T(8,128)(2,1)} %param.15) | copy-start | bytes 3145732
  8.7 28.6 %all-to-all-start = ((s32[64,1,2]{2,1,0:T(1,128)}), s32[64,1,2]{2,1,0:T(1,128)S(1)}, u32[]{:S(2)}, u32[]{:S(2)}) async-start(s32[64,1,2]{2,1,0:T(1,128)} %copy.69), calls=%async_computation | async-start | bytes 65536 | tf_op jit(solution)/shard_map/all_to_all | solution.py:38
  37.3 10.9 %copy-start.5 = (s32[64,1,2]{0,2,1:T(2,128)S(1)}, s32[64,1,2]{0,2,1:T(2,128)}, u32[]{:S(2)}) copy-start(s32[64,1,2]{0,2,1:T(2,128)} %param.19) | copy-start | bytes 1540
  37.3 11.0 %copy-start.9 = (s32[64,1,2]{0,2,1:T(2,128)S(1)}, s32[64,1,2]{0,2,1:T(2,128)}, u32[]{:S(2)}) copy-start(s32[64,1,2]{0,2,1:T(2,128)} %param.20) | copy-start | bytes 1540
  37.3 11.2 %copy-start.4 = (f32[1315,8]{0,1:T(8,128)S(1)}, f32[1315,8]{0,1:T(8,128)}, u32[]{:S(2)}) copy-start(f32[1315,8]{0,1:T(8,128)} %param.16) | copy-start | bytes 126244
  37.3 196.7 %all-to-all-start.1 = ((bf16[64,2,128,256]{3,2,1,0:T(8,128)(2,1)}), bf16[64,2,128,256]{3,2,1,0:T(8,128)(2,1)}, u32[]{:S(2)}, u32[]{:S(2)}) async-start(bf16[64,2,128,256]{3,2,1,0:T(8,128)(2,1)} %broadcast_select_fusion), calls=%async_computation.1 | async-start | bytes 16777216 | tf_op jit(solution)/shard_map/all_to_all | solution.py:37
  47.9 259.2 %all-reduce.2.cloned.1.call-start = ((), (), s32[]{:S(2)}) async-start(), calls=%async_computation.5 | async-start | bytes 1048576 | tf_op jit(solution)/shard_map/psum | solution.py:60
  254.3 52.8 %copy-start.1 = (bf16[512,256]{1,0:T(8,128)(2,1)S(1)}, bf16[512,256]{1,0:T(8,128)(2,1)}, u32[]{:S(2)}) copy-start(bf16[512,256]{1,0:T(8,128)(2,1)} %param.13) | copy-start | bytes 786436
  254.3 52.8 %copy-start.7 = (bf16[256,256]{1,0:T(8,128)(2,1)S(1)}, bf16[256,256]{1,0:T(8,128)(2,1)}, u32[]{:S(2)}) copy-start(bf16[256,256]{1,0:T(8,128)(2,1)} %param.14) | copy-start | bytes 393220
  254.3 52.8 %copy-start.10 = (bf16[512,256]{1,0:T(8,128)(2,1)S(1)}, bf16[512,256]{1,0:T(8,128)(2,1)}, u32[]{:S(2)}) copy-start(bf16[512,256]{1,0:T(8,128)(2,1)} %param.21) | copy-start | bytes 786436
  259.0 1.3 copy-start.2
  324.0 203.1 %all-to-all-start.2 = ((bf16[64,2,128,256]{3,2,1,0:T(8,128)(2,1)}), bf16[64,2,128,256]{3,2,1,0:T(8,128)(2,1)}, u32[]{:S(2)}, u32[]{:S(2)}) async-start(bf16[64,2,128,256]{3,2,1,0:T(8,128)(2,1)} %select_select_fusion), calls=%async_computation.3 | async-start | bytes 16777216 | tf_op jit(solution)/shard_map/all_to_all | solution.py:72
  334.9 8.6 %copy-start.8 = (s32[1,64,2]{1,2,0:T(2,128)S(1)}, s32[1,64,2]{1,2,0:T(2,128)}, u32[]{:S(2)}) copy-start(s32[1,64,2]{1,2,0:T(2,128)} %param.18) | copy-start | bytes 1540
  334.9 8.7 %copy-start.6 = (s32[1,64,2]{1,2,0:T(2,128)S(1)}, s32[1,64,2]{1,2,0:T(2,128)}, u32[]{:S(2)}) copy-start(s32[1,64,2]{1,2,0:T(2,128)} %param.17) | copy-start | bytes 1540
  334.9 234.3 %reduce-scatter.3.cloned.1.call-start = ((), (), s32[]{:S(2)}) async-start(), calls=%async_computation.6 | async-start | bytes 2129920 | tf_op jit(solution)/shard_map/reduce_scatter | solution.py:69
  343.5 227.2 %reduce-scatter.5.cloned.1.call-start = ((), (), s32[]{:S(2)}) async-start(), calls=%async_computation.7 | async-start | bytes 327680 | tf_op jit(solution)/shard_map/reduce_scatter | solution.py:88
  546.0 14.0 %copy-start.3 = (bf16[8,4,32768]{2,1,0:T(4,128)(2,1)S(1)}, bf16[8,4,32768]{2,1,0:T(4,128)(2,1)}, u32[]{:S(2)}) copy-start(bf16[8,4,32768]{2,1,0:T(4,128)(2,1)} %dot_general.47) | copy-start | bytes 6291460
  546.0 101.4 %all-gather.4.cloned.1.call-start = ((), (), s32[]{:S(2)}) async-start(), calls=%async_computation.8 | async-start | bytes 2928640 | tf_op jit(solution)/shard_map/all_gather | solution.py:114
Sparse Core Ops, SparseCore 0:
  262.5 44.5 all-reduce.1
  343.6 169.8 reduce-scatter.2
  546.2 18.7 reduce-scatter.4
  568.1 79.2 all-gather.3
